TPU v7x, 256 devices: a whole 4x4x8 slice. The times are simulated.
256 devices in a mesh: layer: 2 (over core), row: 8 (over z_hi, y), col: 16 (over x, z_lo).
Axes of the slice: x: 4, y: 4, z: 8 (z_hi: 2, z_lo: 4; z = z_hi * 4 + z_lo), core: 2. Of those that a mesh axis runs over, the one named last changes fastest.
Arguments:
- amplitudes: bfloat16 [512, 128, 128], P(('row', 'col')), may hold values from -6 to 6
- integrals: bfloat16 [32768, 128, 128], P(('layer', 'row', 'col')), may hold values from -0.1875 to 0.1875
- amp_index: int32 [4096, 48], P(('layer', 'row', 'col')), may hold values from 0 to 31
- left_index: int32 [4096, 48], P(('layer', 'row', 'col')), may hold values from 0 to 127, as said below
- right_index: int32 [4096, 48], P(('layer', 'row', 'col')), may hold values from 0 to 127, as said below
- dest_col: int32 [2048, 1], P(('row', 'col')), may hold values from 0 to 15; in each aligned block of 16 rows (0 to 15, 16 to 31, ...) at most 2 rows name the same one
- owner_slot: int32 [2048], P(('row', 'col')), may hold values from 0 to 7
Outputs:
- ladder: float32 [1024, 128, 128], P(('row', 'col'))
Inputs may be any that keep to these rules, and one draw needn't show every extreme that they name: `dest_col`: among the 16 result tiles of one index of row and col, no owner column appears more than 2 times, and some column appears exactly 2 times. A term's amplitude tile is number amp_index among the tiles of the devices with the same col index, counted row by row. A term's left and right integral tiles belong to one auxiliary function: left_index // 2 == right_index // 2. right_index // 2 == left_index // 2 for every term.
All inputs are finite; a program needn't handle non-finite values.
Results may differ from a plain program's by a relative error of at most 0.0029.
Values may be sent and summed in bfloat16 or wider, within the bound.
A program may use at most 64 MiB of HBM per device.

v0:
```python
import jax
import jax.numpy as jnp
from jax import lax
from jax.sharding import PartitionSpec as P

OWN = 8
CAP = 2


def select_tiles(stack_flat, picks, count, tile_edge):
    onehot = (picks[:, None] == jnp.arange(count, dtype=jnp.int32)[None, :]).astype(jnp.bfloat16)
    chosen = jnp.dot(onehot, stack_flat, preferred_element_type=jnp.float32).astype(jnp.bfloat16)
    return chosen.reshape(picks.shape[0], tile_edge, tile_edge)


def shards(amplitudes, integrals, amp_index, left_index, right_index, dest_col, owner_slot):
    columns = lax.axis_size("col")
    slot_count = dest_col.shape[0]
    tile_edge = integrals.shape[1]
    gathered = lax.all_gather(amplitudes, "row", axis=0, tiled=True)
    amp_total = gathered.shape[0]
    int_total = integrals.shape[0]
    amp_flat = gathered.reshape(amp_total, tile_edge * tile_edge)
    int_flat = integrals.reshape(int_total, tile_edge * tile_edge)

    def one_slot(operand_list):
        amp_ids, left_ids, right_ids = operand_list
        amp_tiles = select_tiles(amp_flat, amp_ids, amp_total, tile_edge)
        right_tiles = select_tiles(int_flat, right_ids, int_total, tile_edge)
        middle_product = jnp.einsum(
            "tcd,ted->tce", amp_tiles, right_tiles, preferred_element_type=jnp.float32
        ).astype(jnp.bfloat16)
        left_tile_blocks = select_tiles(int_flat, left_ids, int_total, tile_edge)
        return jnp.einsum(
            "dov,dvh->oh", left_tile_blocks, middle_product, preferred_element_type=jnp.float32
        )

    partials = lax.map(one_slot, (amp_index, left_index, right_index))
    target = dest_col[:, 0]
    counter = jnp.arange(slot_count, dtype=jnp.int32)
    earlier = (target[:, None] == target[None, :]) & (counter[None, :] < counter[:, None])
    position_in = jnp.sum(earlier.astype(jnp.int32), axis=1)
    position = target * CAP + position_in
    placing = (position[None, :] == jnp.arange(columns * CAP, dtype=jnp.int32)[:, None]).astype(
        jnp.float32
    )
    buffer = jnp.dot(
        placing,
        partials.reshape(slot_count, tile_edge * tile_edge),
        precision=lax.Precision.HIGHEST,
        preferred_element_type=jnp.float32,
    )
    buffer = buffer.reshape(columns, CAP, tile_edge, tile_edge)
    labels = (
        jnp.full((columns * CAP,), OWN, jnp.int32)
        .at[position]
        .set(owner_slot)
        .reshape(columns, CAP)
    )
    tiles_in, labels_in = (
        lax.all_to_all(buffer, "col", split_axis=0, concat_axis=0, tiled=True),
        lax.all_to_all(labels, "col", split_axis=0, concat_axis=0, tiled=True),
    )
    flattened = tiles_in.reshape(-1, tile_edge * tile_edge)
    owner_mask = (
        labels_in.reshape(-1)[:, None] == jnp.arange(OWN, dtype=jnp.int32)[None, :]
    ).astype(jnp.float32)
    owned_tiles = jnp.dot(
        owner_mask.T, flattened, precision=lax.Precision.HIGHEST, preferred_element_type=jnp.float32
    )
    owned_tiles = lax.psum(owned_tiles, "layer")
    return owned_tiles.reshape(OWN, tile_edge, tile_edge)


def solution(mesh):
    placed = (
        P(("row", "col"), None, None),
        P(("layer", "row", "col"), None, None),
        P(("layer", "row", "col"), None),
        P(("layer", "row", "col"), None),
        P(("layer", "row", "col"), None),
        P(("row", "col"), None),
        P(("row", "col")),
    )
    return jax.shard_map(
        shards, mesh=mesh, in_specs=placed, out_specs=P(("row", "col"), None, None), check_vma=False
    )
```

profile of v0, /device:TPU:1, one launch (start us, length us, event | category | flops | bytes accessed | tf_op | source)
XLA Modules:
  0.0 384.1 jit_solution(10383428219554340299)
XLA Ops:
  10.3 9.0 %all-to-all-start = ((s32[16,1,2]{2,1,0:T(1,128)}), s32[16,1,2]{2,1,0:T(1,128)S(1)}, u32[]{:S(2)}, u32[]{:S(2)}) async-start(s32[16,1,2]{2,1,0:T(1,128)} %bitcast.8), calls=%async_computation | async-start | bytes 16384 | tf_op jit(solution)/shard_map/all_to_all | solution.py:62
  19.3 7.7 %copy.44 = bf16[16,8,128,128]{3,1,2,0:T(8,128)(2,1)} copy(bf16[16,8,128,128]{3,2,1,0:T(8,128)(2,1)} %bitcast.108) | data formatting | bytes 8388608
  27.0 47.3 %all-gather.2.cloned.1.call-done = bf16[32,128,128]{2,1,0:T(8,128)(2,1)} async-done(((bf16[4,128,128]{2,1,0:T(8,128)(2,1)}), bf16[32,128,128]{2,1,0:T(8,128)(2,1)}) %all-gather.2.cloned.1.call-update) | async-done | bytes 1048592 | tf_op jit(solution)/shard_map/all_gather | solution.py:20
  77.2 210.3 %while.10 = (s32[]{:T(128)}, f32[16,128,128]{2,1,0:T(8,128)}, s32[16,48]{1,0:T(8,128)}, bf16[128,16384]{1,0:T(8,128)(2,1)}, s32[16,48]{1,0:T(8,128)}, /*index=5*...) while((s32[]{:T(128)}, f32[16,128,128]{2,1,0:T(8,128)}, s32[16,48]{1,0:T(8,128)}, ...), condition=%wide.region_3.4_spmd, body=%wide.region_2.3_spmd.sunk | while | flops 858797568 | bytes 45156664 | solution.py:38
  86.7 3.7 fusion.58
  91.1 2.9 fusion.54
  99.8 3.7 fusion.58
  113.0 3.7 fusion.58
  117.3 2.9 fusion.54
  126.1 3.7 fusion.58
  130.5 2.9 fusion.54
  139.3 3.7 fusion.58
  152.4 3.7 fusion.58
  156.8 2.9 fusion.54
  165.6 3.7 fusion.58
  169.9 2.9 fusion.54
  178.7 3.7 fusion.58
  183.1 2.9 fusion.54
  191.9 3.7 fusion.58
  205.0 3.7 fusion.58
  209.4 2.9 fusion.54
  218.1 3.7 fusion.58
  222.5 2.9 fusion.54
  231.3 3.7 fusion.58
  235.7 2.9 fusion.54
  244.4 3.7 fusion.58
  257.6 3.7 fusion.58
  270.7 3.7 fusion.58
  283.9 3.7 fusion.58
  292.2 4.5 %all-to-all-start.1 = ((f32[16,2,128,128]{3,2,1,0:T(8,128)}), f32[16,2,128,128]{3,2,1,0:T(8,128)S(1)}, u32[]{:S(2)}, u32[]{:S(2)}) async-start(f32[16,2,128,128]{3,2,1,0:T(8,128)} %copy.18), calls=%async_computation.1 | async-start | bytes 4194304 | tf_op jit(solution)/shard_map/all_to_all | solution.py:61
  298.2 48.2 %all-to-all-done.1 = f32[16,2,128,128]{3,2,1,0:T(8,128)S(1)} async-done(((f32[16,2,128,128]{3,2,1,0:T(8,128)}), f32[16,2,128,128]{3,2,1,0:T(8,128)S(1)}, u32[]{:S(2)}, u32[]{:S(2)}) %all-to-all-start.1) | async-done | bytes 2097184 | tf_op jit(solution)/shard_map/all_to_all | solution.py:61
  349.4 26.0 %all-reduce.2.cloned.1.call-done = f32[8,128,128]{2,1,0:T(8,128)} async-done(((f32[8,128,128]{2,1,0:T(8,128)}), f32[8,128,128]{2,1,0:T(8,128)}) %all-reduce.2.cloned.1.call-update) | async-done | bytes 524304 | tf_op jit(solution)/shard_map/psum | solution.py:71
  (174 shorter events, 142.3 us)
Async XLA Ops:
  6.5 67.8 %all-gather.2.cloned.1.call-start = ((), (), s32[]{:S(2)}) async-start(), calls=%async_computation.2 | async-start | bytes 1179648 | tf_op jit(solution)/shard_map/all_gather | solution.py:20
  10.3 281.9 %all-to-all-start = ((s32[16,1,2]{2,1,0:T(1,128)}), s32[16,1,2]{2,1,0:T(1,128)S(1)}, u32[]{:S(2)}, u32[]{:S(2)}) async-start(s32[16,1,2]{2,1,0:T(1,128)} %bitcast.8), calls=%async_computation | async-start | bytes 16384 | tf_op jit(solution)/shard_map/all_to_all | solution.py:62
  19.3 7.7 %copy-start.1 = (s32[16,1]{0,1:T(1,128)S(1)}, s32[16,1]{0,1:T(1,128)}, u32[]{:S(2)}) copy-start(s32[16,1]{0,1:T(1,128)} %param.14) | copy-start | bytes 196
  81.2 3.1 copy-start
  94.4 3.1 copy-start
  107.5 3.1 copy-start
  120.7 3.1 copy-start
  133.8 3.1 copy-start
  147.0 3.1 copy-start
  160.1 3.1 copy-start
  173.3 3.1 copy-start
  186.4 3.1 copy-start
  199.6 3.1 copy-start
  212.7 3.1 copy-start
  225.8 3.1 copy-start
  239.0 3.1 copy-start
  252.1 3.1 copy-start
  265.3 3.1 copy-start
  278.4 3.1 copy-start
  292.2 54.3 %all-to-all-start.1 = ((f32[16,2,128,128]{3,2,1,0:T(8,128)}), f32[16,2,128,128]{3,2,1,0:T(8,128)S(1)}, u32[]{:S(2)}, u32[]{:S(2)}) async-start(f32[16,2,128,128]{3,2,1,0:T(8,128)} %copy.18), calls=%async_computation.1 | async-start | bytes 4194304 | tf_op jit(solution)/shard_map/all_to_all | solution.py:61
  296.7 78.7 %all-reduce.2.cloned.1.call-start = ((), (), s32[]{:S(2)}) async-start(), calls=%async_computation.3 | async-start | bytes 1048576 | tf_op jit(solution)/shard_map/psum | solution.py:71
Sparse Core Ops, SparseCore 0:
  10.0 64.2 all-gather.1
  349.6 25.8 all-reduce.1
where the time goes:
time: 386 us; the launch traced here: 384 us
  matrix products  153 us (40%)
  waiting for transfers between devices  122 us (32%)
  local copies, waits for them, and re-layouts  78.2 us (20%)
  starting transfers between devices  13.8 us (4%)
  between operations  13.5 us (3%)
    dot_general x48, matrix products, select_tiles(): jnp.dot(onehot, stack_flat, preferred_element_type=jnp.float32)  90.2 us
    dot_general x16, matrix products, one_slot(): jnp.einsum('dov,dvh->oh', left_tile_blocks, middle_product, preferred_ele...  58.6 us
    all_to_all x1, waiting for transfers between devices, shards(): lax.all_to_all(buffer, 'col', split_axis=0, concat_axis=0, tiled=True)  48.2 us
    all_gather x1, waiting for transfers between devices, shards(): gathered = lax.all_gather(amplitudes, 'row', axis=0, tiled=True)  47.3 us
    while x80, local copies, waits for them, and re-layouts  38.3 us
    psum x1, waiting for transfers between devices, shards(): owned_tiles = lax.psum(owned_tiles, 'layer')  26 us
    eq x32, local copies, waits for them, and re-layouts, select_tiles(): picks[:, None] == jnp.arange(count, dtype=jnp.int32)[None, :]  22.5 us
    unnamed x5, local copies, waits for them, and re-layouts  12.5 us
  transfers between devices with their start and end apart: 4, of which 3 were waited for; matrix products, arithmetic and copies ran while one was open for 59% of the time, Pallas kernels for 0%

commit v1 on v0

--- a/solution.py
+++ b/solution.py
@@ -68,7 +68,7 @@
     owned_tiles = jnp.dot(
         owner_mask.T, flattened, precision=lax.Precision.HIGHEST, preferred_element_type=jnp.float32
     )
-    owned_tiles = lax.psum(owned_tiles, "layer")
+    owned_tiles = jnp.sum(jax.lax.all_gather(owned_tiles, axis_name="layer"), axis=0)
     return owned_tiles.reshape(OWN, tile_edge, tile_edge)
 
 

time: 386 us -> 372 us (0.964)
  waiting for transfers between devices: 122 us -> 107 us
    psum x1 -> x0, waiting for transfers between devices: 26 us -> none  [shards(): owned_tiles = lax.psum(owned_tiles, 'layer')]
    all_gather x0 -> x1, waiting for transfers between devices: none -> 10.9 us  [shards(): jax.lax.all_gather(owned_tiles, axis_name='layer')]
  transfers between devices with their start and end apart: 4 -> 4, of which waited for: 3 -> 3; matrix products, arithmetic and copies ran while one was open for 59% -> 62% of each run, Pallas kernels for 0% -> 0%
where the time goes in v1:
time: 372 us; the launch traced here: 369 us
  matrix products  154 us (41%)
  waiting for transfers between devices  107 us (29%)
  local copies, waits for them, and re-layouts  76.3 us (21%)
  starting transfers between devices  13.8 us (4%)
  between operations  13.5 us (4%)
    dot_general x48, matrix products, select_tiles(): jnp.dot(onehot, stack_flat, preferred_element_type=jnp.float32)  90.2 us
    dot_general x16, matrix products, one_slot(): jnp.einsum('dov,dvh->oh', left_tile_blocks, middle_product, preferred_ele...  58.6 us
    all_to_all x1, waiting for transfers between devices, shards(): lax.all_to_all(buffer, 'col', split_axis=0, concat_axis=0, tiled=True)  48.2 us
    all_gather x1, waiting for transfers between devices, shards(): gathered = lax.all_gather(amplitudes, 'row', axis=0, tiled=True)  47.3 us
    while x80, local copies, waits for them, and re-layouts  38.3 us
    eq x32, local copies, waits for them, and re-layouts, select_tiles(): picks[:, None] == jnp.arange(count, dtype=jnp.int32)[None, :]  22.5 us
    unnamed x5, local copies, waits for them, and re-layouts  11.5 us
    all_gather x1, waiting for transfers between devices, shards(): jax.lax.all_gather(owned_tiles, axis_name='layer')  10.9 us
  transfers between devices with their start and end apart: 4, of which 3 were waited for; matrix products, arithmetic and copies ran while one was open for 62% of the time, Pallas kernels for 0%

profile of v1, /device:TPU:1, one launch (start us, length us, event | category | flops | bytes accessed | tf_op | source)
XLA Modules:
  0.0 369.3 jit_solution(8995333401152293739)
XLA Ops:
  10.3 9.0 %all-to-all-start = ((s32[16,1,2]{2,1,0:T(1,128)}), s32[16,1,2]{2,1,0:T(1,128)S(1)}, u32[]{:S(2)}, u32[]{:S(2)}) async-start(s32[16,1,2]{2,1,0:T(1,128)} %bitcast.8), calls=%async_computation | async-start | bytes 16384 | tf_op jit(solution)/shard_map/all_to_all | solution.py:62
  19.3 7.7 %copy.40 = bf16[16,8,128,128]{3,1,2,0:T(8,128)(2,1)} copy(bf16[16,8,128,128]{3,2,1,0:T(8,128)(2,1)} %bitcast.110) | data formatting | bytes 8388608
  27.0 47.3 %all-gather.4.cloned.1.call-done = bf16[32,128,128]{2,1,0:T(8,128)(2,1)} async-done(((bf16[4,128,128]{2,1,0:T(8,128)(2,1)}), bf16[32,128,128]{2,1,0:T(8,128)(2,1)}) %all-gather.4.cloned.1.call-update) | async-done | bytes 1048592 | tf_op jit(solution)/shard_map/all_gather | solution.py:20
  77.2 210.3 %while.10 = (s32[]{:T(128)}, f32[16,128,128]{2,1,0:T(8,128)}, s32[16,48]{1,0:T(8,128)}, bf16[128,16384]{1,0:T(8,128)(2,1)}, s32[16,48]{1,0:T(8,128)}, /*index=5*...) while((s32[]{:T(128)}, f32[16,128,128]{2,1,0:T(8,128)}, s32[16,48]{1,0:T(8,128)}, ...), condition=%wide.region_3.4_spmd, body=%wide.region_2.3_spmd.sunk | while | flops 858797568 | bytes 45156664 | solution.py:38
  86.7 3.7 fusion.55
  91.1 2.9 fusion.51
  99.8 3.7 fusion.55
  113.0 3.7 fusion.55
  117.3 2.9 fusion.51
  126.1 3.7 fusion.55
  130.5 2.9 fusion.51
  139.3 3.7 fusion.55
  152.4 3.7 fusion.55
  156.8 2.9 fusion.51
  165.6 3.7 fusion.55
  169.9 2.9 fusion.51
  178.7 3.7 fusion.55
  183.1 2.9 fusion.51
  191.9 3.7 fusion.55
  205.0 3.7 fusion.55
  209.4 2.9 fusion.51
  218.1 3.7 fusion.55
  222.5 2.9 fusion.51
  231.3 3.7 fusion.55
  235.7 2.9 fusion.51
  244.4 3.7 fusion.55
  257.6 3.7 fusion.55
  270.7 3.7 fusion.55
  283.9 3.7 fusion.55
  292.2 4.5 %all-to-all-start.1 = ((f32[16,2,128,128]{3,2,1,0:T(8,128)}), f32[16,2,128,128]{3,2,1,0:T(8,128)S(1)}, u32[]{:S(2)}, u32[]{:S(2)}) async-start(f32[16,2,128,128]{3,2,1,0:T(8,128)} %copy.15), calls=%async_computation.1 | async-start | bytes 4194304 | tf_op jit(solution)/shard_map/all_to_all | solution.py:61
  298.2 48.2 %all-to-all-done.1 = f32[16,2,128,128]{3,2,1,0:T(8,128)S(1)} async-done(((f32[16,2,128,128]{3,2,1,0:T(8,128)}), f32[16,2,128,128]{3,2,1,0:T(8,128)S(1)}, u32[]{:S(2)}, u32[]{:S(2)}) %all-to-all-start.1) | async-done | bytes 2097184 | tf_op jit(solution)/shard_map/all_to_all | solution.py:61
  349.3 10.9 %all-gather.6.cloned.1.call-done = f32[16,16384]{1,0:T(8,128)} async-done(((f32[8,16384]{1,0:T(8,128)}), f32[16,16384]{1,0:T(8,128)}) %all-gather.6.cloned.1.call-update) | async-done | bytes 1048592 | tf_op jit(solution)/shard_map/all_gather | solution.py:71
  (174 shorter events, 142.5 us)
Async XLA Ops:
  6.5 67.8 %all-gather.4.cloned.1.call-start = ((), (), s32[]{:S(2)}) async-start(), calls=%async_computation.2 | async-start | bytes 1179648 | tf_op jit(solution)/shard_map/all_gather | solution.py:20
  10.3 281.9 %all-to-all-start = ((s32[16,1,2]{2,1,0:T(1,128)}), s32[16,1,2]{2,1,0:T(1,128)S(1)}, u32[]{:S(2)}, u32[]{:S(2)}) async-start(s32[16,1,2]{2,1,0:T(1,128)} %bitcast.8), calls=%async_computation | async-start | bytes 16384 | tf_op jit(solution)/shard_map/all_to_all | solution.py:62
  19.3 7.7 %copy-start.1 = (s32[16,1]{0,1:T(1,128)S(1)}, s32[16,1]{0,1:T(1,128)}, u32[]{:S(2)}) copy-start(s32[16,1]{0,1:T(1,128)} %param.14) | copy-start | bytes 196
  81.2 3.1 copy-start
  94.4 3.1 copy-start
  107.5 3.1 copy-start
  120.7 3.1 copy-start
  133.8 3.1 copy-start
  147.0 3.1 copy-start
  160.1 3.1 copy-start
  173.3 3.1 copy-start
  186.4 3.1 copy-start
  199.6 3.1 copy-start
  212.7 3.1 copy-start
  225.8 3.1 copy-start
  239.0 3.1 copy-start
  252.1 3.1 copy-start
  265.3 3.1 copy-start
  278.4 3.1 copy-start
  292.2 54.3 %all-to-all-start.1 = ((f32[16,2,128,128]{3,2,1,0:T(8,128)}), f32[16,2,128,128]{3,2,1,0:T(8,128)S(1)}, u32[]{:S(2)}, u32[]{:S(2)}) async-start(f32[16,2,128,128]{3,2,1,0:T(8,128)} %copy.15), calls=%async_computation.1 | async-start | bytes 4194304 | tf_op jit(solution)/shard_map/all_to_all | solution.py:61
  296.7 63.4 %all-gather.6.cloned.1.call-start = ((), (), s32[]{:S(2)}) async-start(), calls=%async_computation.3 | async-start | bytes 1572864 | tf_op jit(solution)/shard_map/all_gather | solution.py:71
Sparse Core Ops, SparseCore 0:
  10.0 64.2 all-gather.3
  349.4 10.6 all-gather.5
